TPU v7x, 32 devices: a whole 2x2x4 slice. The times are simulated.
32 devices in a mesh: rep: 8 (over z, y), tp: 4 (over x, core).
Axes of the slice: x: 2, y: 2, z: 4, core: 2. Of those that a mesh axis runs over, the one named last changes fastest.
Arguments:
- image_grads: bfloat16 [32, 48, 1280], P('rep', 'tp'), may hold values from -6 to 6
- dest_rank: int32 [32], P('rep'), may hold values from 0 to 7, as said below
- dest_slot: int32 [32], P('rep'), may hold values from 0 to 7, as said below
- saved_inputs: bfloat16 [64, 48, 1280], P('rep'), may hold values from -6 to 6
- up_weight: bfloat16 [1280, 5120], P(None, 'tp'), may hold values from -0.15625 to 0.15625
- down_weight: bfloat16 [5120, 1280], P('tp'), may hold values from -0.078125 to 0.078125
- norm_gain: float32 [1280], replicated, may hold values from 0.25 to 1.75
Outputs:
- input_grads: bfloat16 [64, 48, 1280], P('rep', 'tp')
- up_grads: float32 [1280, 5120], P('rep', 'tp')
- down_grads: float32 [5120, 1280], P('tp', 'rep')
- gain_grads: float32 [1280], replicated
Inputs may be any that keep to these rules, and one draw needn't show every extreme that they name: `dest_rank`: the images of one index of rep go to different owners; each owner receives at most 8 images, and some owner receives exactly 8 in every draw. `dest_slot`: the images that one owner receives have distinct slots 0, 1, ... up to their count less one; other slots hold no image.
All inputs are finite; a program needn't handle non-finite values.
Results may differ from a plain program's by a relative error of at most 0.015.
Values may be sent and summed in bfloat16 or wider, within the bound.
No kernel may reach another device: no remote copies, remote signals or barrier semaphores. Data moves between devices by JAX's collectives and lax.ppermute only.
A program may use at most 128 MiB of HBM per device.

v0:
```python
import jax
import jax.numpy as jnp
from jax import lax
from jax.sharding import PartitionSpec as P

epsilon = 1e-05
gelu_c = 0.7978845608028654
gelu_a = 0.044715


def gelu_value(preact):
    inner = jnp.tanh(gelu_c * (preact + gelu_a * preact**3))
    return 0.5 * preact * (1.0 + inner)


def gelu_slope(preact):
    inner = jnp.tanh(gelu_c * (preact + gelu_a * preact**3))
    return 0.5 * (1.0 + inner) + 0.5 * preact * (1.0 - inner * inner) * gelu_c * (
        1.0 + 3.0 * gelu_a * preact * preact
    )


def outbound(images, dest_rank, dest_slot, groups, capacity):
    rank_ids = jnp.arange(groups, dtype=jnp.int32)
    one_hot = dest_rank[None, :] == rank_ids[:, None]
    packed = jnp.einsum(
        "ek,kpd->epd", one_hot.astype(jnp.bfloat16), images, preferred_element_type=jnp.float32
    ).astype(jnp.bfloat16)
    present = jnp.any(one_hot, axis=1)
    slot_sent = jnp.sum(jnp.where(one_hot, dest_slot[None, :], 0), axis=1) + jnp.where(
        present, 0, capacity
    )
    return (packed, slot_sent)


def compact(inbound, slot_recv, capacity):
    slot_ids = jnp.arange(capacity, dtype=jnp.int32)
    picker = (slot_recv[None, :] == slot_ids[:, None]).astype(jnp.bfloat16)
    return jnp.einsum("ce,epd->cpd", picker, inbound, preferred_element_type=jnp.float32).astype(
        jnp.bfloat16
    )


def local(image_grads, dest_rank, dest_slot, saved_inputs, up_weight, down_weight, norm_gain):
    groups = lax.axis_size("rep")
    capacity = saved_inputs.shape[0]
    patches = saved_inputs.shape[1]
    width = saved_inputs.shape[2]
    slab = image_grads.shape[1]
    packed, slot_sent = outbound(image_grads, dest_rank, dest_slot, groups, capacity)
    inbound, slot_recv = (
        lax.all_to_all(packed, "rep", split_axis=0, concat_axis=0, tiled=True),
        lax.all_to_all(slot_sent, "rep", split_axis=0, concat_axis=0, tiled=True),
    )
    routed = lax.all_gather(compact(inbound, slot_recv, capacity), "tp", axis=1, tiled=True)
    rows = capacity * patches
    grads = routed.reshape(rows, width)
    values = saved_inputs.reshape(rows, width).astype(jnp.float32)
    mean_v = jnp.mean(values, axis=1, keepdims=True)
    var_v = jnp.mean((values - mean_v) ** 2, axis=1, keepdims=True)
    inv_std = 1.0 / jnp.sqrt(var_v + epsilon)
    centred = (values - mean_v) * inv_std
    normed = (centred * norm_gain[None, :]).astype(jnp.bfloat16)
    preact = jnp.dot(normed, up_weight, preferred_element_type=jnp.float32)
    hidden = gelu_value(preact).astype(jnp.bfloat16)
    grad_hidden = jnp.dot(grads, down_weight.T, preferred_element_type=jnp.float32)
    grad_pre = (grad_hidden * gelu_slope(preact)).astype(jnp.bfloat16)
    down_local = jnp.dot(hidden.T, grads, preferred_element_type=jnp.float32)
    up_local = jnp.dot(normed.T, grad_pre, preferred_element_type=jnp.float32)
    partial_normed = jnp.dot(grad_pre, up_weight.T, preferred_element_type=jnp.float32)
    up_grads, down_grads = (
        lax.psum_scatter(
            up_local.astype(jnp.bfloat16), "rep", scatter_dimension=0, tiled=True
        ).astype(jnp.float32),
        lax.psum_scatter(
            down_local.astype(jnp.bfloat16), "rep", scatter_dimension=1, tiled=True
        ).astype(jnp.float32),
    )
    start = lax.axis_index("tp") * slab
    grad_normed = lax.psum(partial_normed.astype(jnp.bfloat16), "tp").astype(jnp.float32)
    gain_grads = lax.psum(jnp.sum(grad_normed * centred, axis=0), "rep")
    scaled = grad_normed * norm_gain[None, :]
    first = jnp.mean(scaled, axis=1, keepdims=True)
    second = jnp.mean(scaled * centred, axis=1, keepdims=True)
    result = grads.astype(jnp.float32) + inv_std * (scaled - first - centred * second)
    result = result.reshape(capacity, patches, width)
    input_grads = lax.dynamic_slice_in_dim(result, start, slab, 1).astype(jnp.bfloat16)
    return (input_grads, up_grads, down_grads, gain_grads)


def solution(mesh):
    in_specs = (
        P("rep", "tp", None),
        P("rep"),
        P("rep"),
        P("rep", None, None),
        P(None, "tp"),
        P("tp", None),
        P(),
    )
    out_specs = (P("rep", "tp", None), P("rep", "tp"), P("tp", "rep"), P())
    return jax.shard_map(local, mesh=mesh, in_specs=in_specs, out_specs=out_specs, check_vma=False)
```

profile of v0, /device:TPU:0, one launch (start us, length us, event | category | flops | bytes accessed | tf_op | source)
XLA Modules:
  0.0 227.4 jit_solution(4812168266985921151)
XLA Ops:
  8.0 0.9 fusion.26
  8.9 0.9 select_reduce_fusion
  10.5 7.3 %all-to-all-start = ((s32[8,1,1]{2,1,0:T(1,128)}), s32[8,1,1]{2,1,0:T(1,128)S(1)}, u32[]{:S(2)}, u32[]{:S(2)}) async-start(s32[8,1,1]{2,1,0:T(1,128)} %copy.19), calls=%async_computation | async-start | bytes 8192 | tf_op jit(solution)/shard_map/all_to_all | solution.py:53
  17.8 1.4 convert_reduce_fusion
  19.3 1.6 multiply_reduce_fusion
  21.4 2.5 %multiply_convert_fusion.1 = bf16[384,1280]{1,0:T(8,128)(2,1)} fusion(bf16[8,48,1280]{2,1,0:T(8,128)(2,1)} %param.10, f32[1280]{0:T(1024)S(1)} %copy-done.5, f32[384]{0:T(512)S(1)} %div.18, f32[384]{0:T(512)S(1)} %sqrt.6), kind=kLoop, calls=%fused_computation.29 | loop fusion | flops 2457600 | bytes 1974272 | tf_op jit(solution)/shard_map/convert_element_type | solution.py:63
  24.7 6.0 %all-to-all-start.1 = ((bf16[8,12,1280]{2,1,0:T(8,128)(2,1)}), bf16[8,12,1280]{2,1,0:T(8,128)(2,1)}, u32[]{:S(2)}, u32[]{:S(2)}) async-start(bf16[8,12,1280]{2,1,0:T(8,128)(2,1)} %copy.20), calls=%async_computation.1 | async-start | bytes 655360 | tf_op jit(solution)/shard_map/all_to_all | solution.py:52
  30.7 4.0 %fusion.33 = f32[384,1280]{1,0:T(8,128)} fusion(bf16[384,1280]{1,0:T(8,128)(2,1)} %multiply_convert_fusion.1, bf16[1280,1280]{1,0:T(8,128)(2,1)S(1)} %copy-done), kind=kOutput, calls=%fused_computation.56 | convolution fusion | flops 1258291200 | bytes 6225920 | tf_op jit(solution)/shard_map/dot_general | solution.py:64
  34.9 5.6 %all-to-all-done.1 = bf16[8,12,1280]{2,1,0:T(8,128)(2,1)} async-done(((bf16[8,12,1280]{2,1,0:T(8,128)(2,1)}), bf16[8,12,1280]{2,1,0:T(8,128)(2,1)}, u32[]{:S(2)}, u32[]{:S(2)}) %all-to-all-start.1) | async-done | bytes 245792 | tf_op jit(solution)/shard_map/all_to_all | solution.py:52
  40.5 1.3 convolution_convert_fusion.3
  41.9 9.7 %all_gather.3 = bf16[8,48,1280]{2,0,1:T(8,128)(2,1)S(1)} all-gather(bf16[8,12,1280]{2,0,1:T(8,128)(2,1)S(1)} %convolution_convert_fusion.3), channel_id=1, replica_groups=mesh['rep'=8,'tp'=4] {'tp'}, dimensions={1}, use_global_device_ids=true | all-gather | bytes 1228800 | tf_op jit(solution)/shard_map/all_gather | solution.py:55
  51.7 3.8 %fusion = bf16[384,1280]{1,0:T(8,128)(2,1)S(1)} fusion(bf16[384,1280]{1,0:T(8,128)(2,1)S(1)} %bitcast.33, bf16[1280,1280]{1,0:T(8,128)(2,1)S(1)} %copy-done.7, f32[384,1280]{1,0:T(8,128)} %fusion.33), kind=kOutput, calls=%fused_computation.5 | convolution fusion | flops 1267630080 | bytes 7208960 | tf_op jit(solution)/shard_map/dot_general | solution.py:66
  55.6 0.9 copy-done.8
  56.5 2.4 %convolution_convert_fusion.2 = bf16[384,1280]{1,0:T(8,128)(2,1)} fusion(bf16[384,1280]{1,0:T(8,128)(2,1)S(1)} %fusion, bf16[1280,1280]{1,0:T(8,128)(2,1)S(1)} %copy-done), kind=kOutput, calls=%fused_computation.6 | convolution fusion | flops 1258782720 | bytes 5242880 | tf_op jit(solution)/shard_map/dot_general | solution.py:70
  59.0 5.1 %convolution_convert_fusion.1 = bf16[1280,1280]{1,0:T(8,128)(2,1)} fusion(bf16[384,1280]{1,0:T(8,128)(2,1)} %multiply_convert_fusion.1, bf16[384,1280]{1,0:T(8,128)(2,1)} %copy-done.8), kind=kOutput, calls=%fused_computation.1 | convolution fusion | flops 1259929600 | bytes 5242880 | tf_op jit(solution)/shard_map/dot_general | solution.py:69
  64.4 5.5 %convolution_convert_fusion = bf16[1280,1280]{0,1:T(8,128)(2,1)} fusion(bf16[384,1280]{1,0:T(8,128)(2,1)} %bitcast.34, f32[384,1280]{1,0:T(8,128)} %fusion.33), kind=kOutput, calls=%fused_computation | convolution fusion | flops 1264353280 | bytes 6225920 | tf_op jit(solution)/shard_map/dot_general | solution.py:68
  69.9 23.6 %all-reduce.2.cloned.1.call-done = bf16[384,1280]{1,0:T(8,128)(2,1)} async-done(((bf16[384,1280]{1,0:T(8,128)(2,1)}), bf16[384,1280]{1,0:T(8,128)(2,1)}) %all-reduce.2.cloned.1.call-update) | async-done | bytes 983056 | tf_op jit(solution)/shard_map/psum | solution.py:80
  93.5 2.6 %fusion.8 = (f32[1280]{0:T(1024)S(1)}, f32[384]{0:T(512)S(1)}, f32[384]{0:T(512)S(1)}) fusion(bf16[384,1280]{1,0:T(8,128)(2,1)} %all-reduce.2.cloned.1.call-done, bf16[8,48,1280]{2,1,0:T(8,128)(2,1)} %param.10, f32[384]{0:T(512)S(1)} %div.18, f32[384]{0:T(512)S(1)} %sqrt.6, f32[1280]{0:T(1024)S(1)} %copy-done.5), kind=kLoop, calls=%fused_computation.18 | loop fusion | flops 4913152 | bytes 1982464 | tf_op jit(solution)/shard_map/reduce_sum | solution.py:81
  96.1 2.1 fusion.6
  99.0 22.1 %psum.15 = f32[1280]{0:T(1024)} all-reduce(f32[1280]{0:T(1024)S(1)} %get-tuple-element.4), channel_id=1, replica_groups=mesh['rep'=8,'tp'=4] {'rep'}, use_global_device_ids=true, to_apply=%region_10.11 | all-reduce | flops 1280 | bytes 10240 | tf_op jit(solution)/shard_map/psum | solution.py:81
  121.2 18.0 %reduce-scatter.3.cloned.1.call-done = bf16[160,1280]{1,0:T(8,128)(2,1)} async-done(((bf16[1280,1280]{1,0:T(8,128)(2,1)}), bf16[160,1280]{1,0:T(8,128)(2,1)}) %reduce-scatter.3.cloned.1.call-update) | async-done | bytes 409616 | tf_op jit(solution)/shard_map/reduce_scatter | solution.py:72
  139.2 1.9 convert_element_type.63
  141.1 76.9 %reduce-scatter.5.cloned.1.call-done = bf16[1280,160]{0,1:T(8,128)(2,1)} async-done(((bf16[1280,1280]{0,1:T(8,128)(2,1)}), bf16[1280,160]{0,1:T(8,128)(2,1)}) %reduce-scatter.5.cloned.1.call-update) | async-done | bytes 409616 | tf_op jit(solution)/shard_map/reduce_scatter | solution.py:75
  218.0 1.9 convert_element_type.66
  (37 shorter events, 3.6 us)
Async XLA Ops:
  8.0 22.7 %copy-start = (bf16[1280,1280]{1,0:T(8,128)(2,1)S(1)}, bf16[1280,1280]{1,0:T(8,128)(2,1)}, u32[]{:S(2)}) copy-start(bf16[1280,1280]{1,0:T(8,128)(2,1)} %param.11) | copy-start | bytes 9830404
  8.0 13.0 %copy-start.6 = (s32[4]{0:T(128)S(1)}, s32[4]{0:T(128)}, u32[]{:S(2)}) copy-start(s32[4]{0:T(128)} %param.8) | copy-start | bytes 52
  8.0 13.0 %copy-start.4 = (bf16[4,12,1280]{2,0,1:T(4,128)(2,1)S(1)}, bf16[4,12,1280]{2,0,1:T(4,128)(2,1)}, u32[]{:S(2)}) copy-start(bf16[4,12,1280]{2,0,1:T(4,128)(2,1)} %param.7) | copy-start | bytes 368644
  8.0 13.4 %copy-start.5 = (f32[1280]{0:T(1024)S(1)}, f32[1280]{0:T(1024)}, u32[]{:S(2)}) copy-start(f32[1280]{0:T(1024)} %param.13) | copy-start | bytes 15364
  10.5 14.2 %all-to-all-start = ((s32[8,1,1]{2,1,0:T(1,128)}), s32[8,1,1]{2,1,0:T(1,128)S(1)}, u32[]{:S(2)}, u32[]{:S(2)}) async-start(s32[8,1,1]{2,1,0:T(1,128)} %copy.19), calls=%async_computation | async-start | bytes 8192 | tf_op jit(solution)/shard_map/all_to_all | solution.py:53
  24.7 15.8 %all-to-all-start.1 = ((bf16[8,12,1280]{2,1,0:T(8,128)(2,1)}), bf16[8,12,1280]{2,1,0:T(8,128)(2,1)}, u32[]{:S(2)}, u32[]{:S(2)}) async-start(bf16[8,12,1280]{2,1,0:T(8,128)(2,1)} %copy.20), calls=%async_computation.1 | async-start | bytes 655360 | tf_op jit(solution)/shard_map/all_to_all | solution.py:52
  30.7 62.8 %all-reduce.2.cloned.1.call-start = ((), (), s32[]{:S(2)}) async-start(), calls=%async_computation.4 | async-start | bytes 1966080 | tf_op jit(solution)/shard_map/psum | solution.py:80
  40.5 11.2 %copy-start.7 = (bf16[1280,1280]{1,0:T(8,128)(2,1)S(1)}, bf16[1280,1280]{1,0:T(8,128)(2,1)}, u32[]{:S(2)}) copy-start(bf16[1280,1280]{1,0:T(8,128)(2,1)} %param.12) | copy-start | bytes 9830404
  51.7 3.9 %copy-start.2 = (bf16[8,48,1280]{2,1,0:T(8,128)(2,1)}, bf16[8,48,1280]{2,1,0:T(8,128)(2,1)S(1)}, u32[]{:S(2)}) copy-start(bf16[8,48,1280]{2,1,0:T(8,128)(2,1)S(1)} %copy.22) | copy-start | bytes 2949124
  55.6 1.0 copy-start.8
  59.0 80.2 %reduce-scatter.3.cloned.1.call-start = ((), (), s32[]{:S(2)}) async-start(), calls=%async_computation.5 | async-start | bytes 3686400 | tf_op jit(solution)/shard_map/reduce_scatter | solution.py:72
  64.1 153.9 %reduce-scatter.5.cloned.1.call-start = ((), (), s32[]{:S(2)}) async-start(), calls=%async_computation.6 | async-start | bytes 3686400 | tf_op jit(solution)/shard_map/reduce_scatter | solution.py:75
  93.5 2.6 %copy-start.1 = (bf16[8,48,1280]{2,1,0:T(8,128)(2,1)S(1)}, bf16[8,48,1280]{2,1,0:T(8,128)(2,1)}, u32[]{:S(2)}) copy-start(bf16[8,48,1280]{2,1,0:T(8,128)(2,1)} %param.10) | copy-start | bytes 2949124
  93.5 2.6 %copy-start.3 = (bf16[8,48,1280]{2,1,0:T(8,128)(2,1)S(1)}, bf16[8,48,1280]{2,1,0:T(8,128)(2,1)}, u32[]{:S(2)}) copy-start(bf16[8,48,1280]{2,1,0:T(8,128)(2,1)} %copy-done.2) | copy-start | bytes 2949124
Sparse Core Ops, SparseCore 0:
  59.1 34.3 all-reduce.1
Sparse Core Ops, SparseCore 1:
  64.2 74.9 reduce-scatter.2
  142.6 75.3 reduce-scatter.4
where the time goes:
time: 228 us; the launch traced here: 227 us
  waiting for transfers between devices  124 us (54%)
  blocking collectives  31.8 us (14%)
  matrix products  22.5 us (10%)
  other arithmetic  16.1 us (7%)
  between operations  15.7 us (7%)
  starting transfers between devices  13.6 us (6%)
  local copies, waits for them, and re-layouts  3.62 us (2%)
    reduce_scatter x1, waiting for transfers between devices, local(): lax.psum_scatter(down_local.astype(jnp.bfloat16), 'rep', scatter_dimensio...  76.9 us
    psum x1, waiting for transfers between devices, local(): lax.psum(partial_normed.astype(jnp.bfloat16), 'tp').astype(jnp.float32)  23.6 us
    psum x1, blocking collectives, local(): gain_grads = lax.psum(jnp.sum(grad_normed * centred, axis=0), 'rep')  22.1 us
    reduce_scatter x1, waiting for transfers between devices, local(): lax.psum_scatter(up_local.astype(jnp.bfloat16), 'rep', scatter_dimension=...  18 us
    all_gather x1, blocking collectives, local(): lax.all_gather(compact(inbound, slot_recv, capacity), 'tp', axis=1, tiled...  9.67 us
    all_to_all x1, starting transfers between devices, local(): lax.all_to_all(slot_sent, 'rep', split_axis=0, concat_axis=0, tiled=True)  7.31 us
    all_to_all x1, starting transfers between devices, local(): lax.all_to_all(packed, 'rep', split_axis=0, concat_axis=0, tiled=True)  6 us
    all_to_all x1, waiting for transfers between devices, local(): lax.all_to_all(packed, 'rep', split_axis=0, concat_axis=0, tiled=True)  5.58 us
  transfers between devices with their start and end apart: 5, of which 4 were waited for; matrix products, arithmetic and copies ran while one was open for 13% of the time, Pallas kernels for 0%

commit v1 on v0

--- a/solution.py
+++ b/solution.py
@@ -18,6 +18,26 @@
     return 0.5 * (1.0 + inner) + 0.5 * preact * (1.0 - inner * inner) * gelu_c * (
         1.0 + 3.0 * gelu_a * preact * preact
     )
+
+
+def gelu_both(preact):
+    square = preact * preact
+    inner = jnp.tanh(gelu_c * (preact + gelu_a * preact * square))
+    half = 0.5 * (1.0 + inner)
+    slope = half + 0.5 * preact * (1.0 - inner * inner) * gelu_c * (1.0 + 3.0 * gelu_a * square)
+    return preact * half, slope
+
+
+def matmul(a, b):
+    return jnp.dot(a, b, preferred_element_type=jnp.float32)
+
+
+def matmul_nt(a, b):
+    return lax.dot_general(a, b, (((1,), (1,)), ((), ())), preferred_element_type=jnp.float32)
+
+
+def matmul_tn(a, b):
+    return lax.dot_general(a, b, (((0,), (0,)), ((), ())), preferred_element_type=jnp.float32)
 
 
 def outbound(images, dest_rank, dest_slot, groups, capacity):
@@ -41,7 +61,7 @@
     )
 
 
-def local(image_grads, dest_rank, dest_slot, saved_inputs, up_weight, down_weight, norm_gain):
+def local_reduce(image_grads, dest_rank, dest_slot, saved_inputs, up_weight, down_weight, norm_gain):
     groups = lax.axis_size("rep")
     capacity = saved_inputs.shape[0]
     patches = saved_inputs.shape[1]
@@ -88,7 +108,156 @@
     return (input_grads, up_grads, down_grads, gain_grads)
 
 
+def shift(x, axis, amount):
+    size = lax.axis_size(axis)
+    return lax.ppermute(x, axis, [(i, (i + amount) % size) for i in range(size)])
+
+
+def flip(x, axis, bit):
+    size = lax.axis_size(axis)
+    return lax.ppermute(x, axis, [(i, i ^ bit) for i in range(size)])
+
+
+def spread(block):
+    groups = lax.axis_size("rep")
+    fars = [block] + [shift(block, "rep", 2 * k) for k in range(1, groups // 2)]
+    half = len(fars) // 2
+    one = jnp.concatenate(fars[:half])
+    two = jnp.concatenate(fars[half:])
+    one = jnp.concatenate([one, flip(one, "rep", 1)])
+    two = jnp.concatenate([two, flip(two, "tp", 2)])
+    one_far = flip(one, "tp", 2)
+    two_far = flip(two, "rep", 1)
+    mine = jnp.concatenate([one, one_far, two, two_far])
+    return (mine, flip(mine, "tp", 1))
+
+
+def spread_ids():
+    groups = lax.axis_size("rep")
+    rep = lax.axis_index("rep")
+    tp = lax.axis_index("tp")
+    fars = [((rep - 2 * k) % groups, tp) for k in range(groups // 2)]
+    half = len(fars) // 2
+    one, two = fars[:half], fars[half:]
+    one = one + [(r ^ 1, t) for r, t in one]
+    two = two + [(r, t ^ 2) for r, t in two]
+    mine = one + [(r, t ^ 2) for r, t in one] + two + [(r ^ 1, t) for r, t in two]
+    both = mine + [(r, t ^ 1) for r, t in mine]
+    return jnp.stack([r for r, _ in both]), jnp.stack([t for _, t in both])
+
+
+def sum_everywhere(x):
+    for axis in ("tp", "rep"):
+        bit = 1
+        while bit < lax.axis_size(axis):
+            x = x + flip(x, axis, bit)
+            bit *= 2
+    return x
+
+
+def local_gather(image_grads, dest_rank, dest_slot, saved_inputs, up_weight, down_weight, norm_gain):
+    groups = lax.axis_size("rep")
+    cuts = lax.axis_size("tp")
+    rep = lax.axis_index("rep")
+    tp = lax.axis_index("tp")
+    capacity, patches, width = saved_inputs.shape
+    held, slab = image_grads.shape[:2]
+    rows = capacity * patches
+    share = width // groups
+
+    slot_ids = jnp.arange(capacity, dtype=jnp.int32)
+    owners = jnp.arange(groups, dtype=jnp.int32)
+    goes = dest_rank[None, :] == owners[:, None]
+    code = dest_slot + capacity * jnp.arange(held, dtype=jnp.int32)
+    sent = jnp.sum(jnp.where(goes, code[None, :], 0), axis=1) + jnp.where(
+        jnp.any(goes, axis=1), 0, capacity * held
+    )
+    codes = lax.all_to_all(sent, "rep", split_axis=0, concat_axis=0, tiled=True)
+    from_slot = jnp.where(codes < capacity * held, codes % capacity, capacity)
+    from_place = codes // capacity
+
+    grads_all = spread(image_grads.reshape(held * slab, width))
+
+    values = saved_inputs.reshape(rows, width).astype(jnp.float32)
+    mean_v = jnp.mean(values, axis=1, keepdims=True)
+    var_v = jnp.mean((values - mean_v) ** 2, axis=1, keepdims=True)
+    inv_std = 1.0 / jnp.sqrt(var_v + epsilon)
+    centred = (values - mean_v) * inv_std
+    normed = (centred * norm_gain[None, :]).astype(jnp.bfloat16)
+
+    mine = lax.dynamic_slice_in_dim(normed.reshape(capacity, patches, width), tp * slab, slab, 1)
+    picker = (from_slot[:, None] == slot_ids[None, :]).astype(jnp.bfloat16)
+    packed = jnp.einsum("ec,cpd->epd", picker, mine, preferred_element_type=jnp.float32)
+    inbound = lax.all_to_all(
+        packed.astype(jnp.bfloat16), "rep", split_axis=0, concat_axis=0, tiled=True
+    )
+    unpack = (dest_rank[:, None] == owners[None, :]).astype(jnp.bfloat16)
+    block = jnp.einsum("ke,epd->kpd", unpack, inbound, preferred_element_type=jnp.float32)
+    normed_all = spread(block.astype(jnp.bfloat16).reshape(held * slab, width))
+
+    rep_of, tp_of = spread_ids()
+    row_ids = jnp.arange(rows, dtype=jnp.int32)
+    slot_of_row = row_ids // patches
+    patch_of_row = row_ids % patches
+    here = from_slot[None, :] == slot_of_row[:, None]
+    source_of_row = jnp.sum(jnp.where(here, owners[None, :], 0), axis=1)
+    place_of_row = jnp.sum(jnp.where(here, from_place[None, :], 0), axis=1)
+    tp_of_row = patch_of_row // slab
+    wanted = ((source_of_row * cuts + tp_of_row) * held + place_of_row) * slab + patch_of_row % slab
+    wanted = jnp.where(jnp.any(here, axis=1), wanted, -1)
+    offsets = jnp.arange(held * slab, dtype=jnp.int32)
+    have = ((rep_of * cuts + tp_of)[:, None] * (held * slab) + offsets[None, :]).reshape(-1)
+    select = (wanted[:, None] == have[None, :]).astype(jnp.bfloat16)
+    middle = have.shape[0] // 2
+    grads = (
+        matmul(select[:, :middle], grads_all[0]) + matmul(select[:, middle:], grads_all[1])
+    ).astype(jnp.bfloat16)
+
+    _, slope = gelu_both(matmul(normed, up_weight))
+    grad_pre = (matmul_nt(grads, down_weight) * slope).astype(jnp.bfloat16)
+    partial_normed = matmul_nt(grad_pre, up_weight)
+    gain_grads = sum_everywhere(jnp.sum(partial_normed * centred, axis=0))
+    pieces = partial_normed.reshape(capacity, cuts // 2, 2, slab, width)
+    core = tp % 2
+    across = tp // 2
+    near = lax.dynamic_index_in_dim(pieces, core, 2, False)
+    away = lax.dynamic_index_in_dim(pieces, 1 - core, 2, False).astype(jnp.bfloat16)
+    near = near + flip(away, "tp", 1).astype(jnp.float32)
+    far = lax.dynamic_index_in_dim(near, 1 - across, 1, False).astype(jnp.bfloat16)
+    total = lax.dynamic_index_in_dim(near, across, 1, False)
+    total = total + flip(far, "tp", 2).astype(jnp.float32)
+
+    def own(x):
+        x = x.reshape(capacity, patches, x.shape[-1])
+        return lax.dynamic_slice_in_dim(x, tp * slab, slab, 1)
+
+    centred_own = own(centred)
+    scaled = total * norm_gain
+    first = jnp.mean(scaled, axis=-1, keepdims=True)
+    second = jnp.mean(scaled * centred_own, axis=-1, keepdims=True)
+    input_grads = (
+        own(grads).astype(jnp.float32) + own(inv_std) * (scaled - first - centred_own * second)
+    ).astype(jnp.bfloat16)
+
+    up_grads = down_grads = 0.0
+    for n_rows, g_rows in zip(normed_all, grads_all):
+        value, slope = gelu_both(matmul(n_rows, up_weight))
+        grad_pre = (matmul_nt(g_rows, down_weight) * slope).astype(jnp.bfloat16)
+        hidden = value.astype(jnp.bfloat16)
+        up_grads += matmul_tn(lax.dynamic_slice_in_dim(n_rows, rep * share, share, 1), grad_pre)
+        down_grads += matmul_tn(hidden, lax.dynamic_slice_in_dim(g_rows, rep * share, share, 1))
+    return (input_grads, up_grads, down_grads, gain_grads)
+
+
 def solution(mesh):
+    groups, cuts = mesh.shape["rep"], mesh.shape["tp"]
+
+    def local(*args):
+        image_grads, _, _, _, up_weight, _, _ = args
+        all_rows = image_grads.shape[0] * image_grads.shape[1] * groups * cuts
+        small = all_rows <= 2 * up_weight.shape[1] and cuts == 4 and groups in (4, 8, 16)
+        return (local_gather if small else local_reduce)(*args)
+
     in_specs = (
         P("rep", "tp", None),
         P("rep"),

time: 228 us -> 181 us (0.79)
  waiting for transfers between devices: 124 us -> 21 us
  local copies, waits for them, and re-layouts: 3.62 us -> 39.5 us
  blocking collectives: 31.8 us -> 0 us
  matrix products: 22.5 us -> 53.9 us
  starting transfers between devices: 13.6 us -> 41.6 us
  between operations: 15.7 us -> 0.94 us
  other arithmetic: 16.1 us -> 22.6 us
    reduce_scatter x2 -> x0, waiting for transfers between devices: 94.9 us -> none  [the longest x1 76.9 us: local(): lax.psum_scatter(down_local.astype(jnp.bfloat16), 'rep', scatter_dimensio...]
    ppermute x0 -> x23, starting transfers between devices: none -> 31.9 us  [the longest x17 20.1 us: flip(): return lax.ppermute(x, axis, [(i, i ^ bit) for i in range(size)])]
    dot_general x7 -> x12, matrix products: 22.5 us -> 53.9 us  [the longest x4 25.7 us: matmul_tn(): lax.dot_general(a, b, (((0,), (0,)), ((), ())), preferred_element_type=jn...]
    psum x1 -> x0, waiting for transfers between devices: 23.6 us -> none  [local(): lax.psum(partial_normed.astype(jnp.bfloat16), 'tp').astype(jnp.float32)]
    psum x1 -> x0, blocking collectives: 22.1 us -> none  [local(): gain_grads = lax.psum(jnp.sum(grad_normed * centred, axis=0), 'rep')]
    ppermute x0 -> x23, waiting for transfers between devices: none -> 21 us  [the longest x17 16.1 us: flip(): return lax.ppermute(x, axis, [(i, i ^ bit) for i in range(size)])]
    unnamed x19 -> x55, local copies, waits for them, and re-layouts: 1.76 us -> 17.1 us
    all_gather x1 -> x0, blocking collectives: 9.67 us -> none  [local(): lax.all_gather(compact(inbound, slot_recv, capacity), 'tp', axis=1, tiled...]
  transfers between devices with their start and end apart: 5 -> 25, of which waited for: 4 -> 7; matrix products, arithmetic and copies ran while one was open for 13% -> 60% of each run, Pallas kernels for 0% -> 0%
where the time goes in v1:
time: 181 us; the launch traced here: 180 us
  matrix products  53.9 us (30%)
  starting transfers between devices  41.6 us (23%)
  local copies, waits for them, and re-layouts  39.5 us (22%)
  other arithmetic  22.6 us (12%)
  waiting for transfers between devices  21 us (12%)
    dot_general x4, matrix products, matmul_tn(): lax.dot_general(a, b, (((0,), (0,)), ((), ())), preferred_element_type=jn...  25.7 us
    ppermute x17, starting transfers between devices, flip(): return lax.ppermute(x, axis, [(i, i ^ bit) for i in range(size)])  20.1 us
    dot_general x5, matrix products, matmul(): return jnp.dot(a, b, preferred_element_type=jnp.float32)  18 us
    unnamed x55, local copies, waits for them, and re-layouts  17.1 us
    ppermute x17, waiting for transfers between devices, flip(): return lax.ppermute(x, axis, [(i, i ^ bit) for i in range(size)])  16.1 us
    ppermute x6, starting transfers between devices, shift(): lax.ppermute(x, axis, [(i, (i + amount) % size) for i in range(size)])  11.7 us
    dot_general x1, matrix products, matmul_nt(): lax.dot_general(a, b, (((1,), (1,)), ((), ())), preferred_element_type=jn...  7.73 us
    all_to_all x1, starting transfers between devices, local_gather(): lax.all_to_all(packed.astype(jnp.bfloat16), 'rep', split_axis=0, concat_a...  5.9 us
  transfers between devices with their start and end apart: 25, of which 7 were waited for; matrix products, arithmetic and copies ran while one was open for 60% of the time, Pallas kernels for 0%

profile of v1, /device:TPU:0, one launch (start us, length us, event | category | flops | bytes accessed | tf_op | source)
XLA Modules:
  0.0 179.6 jit_solution(6511891410356751613)
XLA Ops:
  3.3 3.1 %collective-permute-start = (bf16[48,1280]{1,0:T(8,128)(2,1)S(1)}, bf16[48,1280]{1,0:T(8,128)(2,1)}, u32[]{:S(2)}, u32[]{:S(2)}) collective-permute-start(bf16[48,1280]{1,0:T(8,128)(2,1)S(1)} %reshape.792), channel_id=1, source_target_pairs={{0,8},{4,12},{8,16},{12,20},{16,24},{20,28},{24,0},{28,4},{1,9},{5... | collective-permute-start | bytes 368648 | tf_op jit(solution)/shard_map/ppermute | solution.py:113
  6.4 2.6 %collective-permute-start.3 = (bf16[48,1280]{1,0:T(8,128)(2,1)S(1)}, bf16[48,1280]{1,0:T(8,128)(2,1)S(1)}, u32[]{:S(2)}, u32[]{:S(2)}) collective-permute-start(bf16[48,1280]{1,0:T(8,128)(2,1)S(1)} %reshape.792), channel_id=1, source_target_pairs={{0,16},{4,20},{8,24},{12,28},{16,0},{20,4},{24,8},{28,12},{1,17},{... | collective-permute-start | bytes 368648 | tf_op jit(solution)/shard_map/ppermute | solution.py:113
  13.2 3.8 %all-to-all-start = ((s32[8,1,1]{2,1,0:T(1,128)}), s32[8,1,1]{2,1,0:T(1,128)}, u32[]{:S(2)}, u32[]{:S(2)}) async-start(s32[8,1,1]{2,1,0:T(1,128)} %copy.57), calls=%async_computation | async-start | bytes 8192 | tf_op jit(solution)/shard_map/all_to_all | solution.py:175
  19.3 2.8 %copy_convert_fusion = f32[8,48,1280]{2,0,1:T(8,128)} fusion(bf16[8,48,1280]{2,1,0:T(8,128)(2,1)} %param.10), kind=kLoop, calls=%fused_computation.37 | loop fusion | flops 491520 | bytes 2949120 | tf_op jit(solution)/shard_map/convert_element_type | solution.py:181
  26.8 3.5 %copy.61 = f32[8,48,1280]{2,1,0:T(8,128)} copy(f32[8,48,1280]{2,0,1:T(8,128)} %copy_convert_fusion) | data formatting | bytes 3932160 | tf_op jit(solution)/shard_map/convert_element_type | solution.py:181
  32.4 2.7 %fusion.69 = f32[384,1280]{1,0:T(8,128)} fusion(bf16[384,1280]{1,0:T(8,128)(2,1)S(1)} %multiply_convert_fusion.2, bf16[1280,1280]{1,0:T(8,128)(2,1)S(1)} %copy-done), kind=kOutput, calls=%fused_computation.154 | convolution fusion | flops 1258291200 | bytes 6225920 | tf_op jit(solution)/shard_map/dot_general | solution.py:32
  38.8 5.9 %all-to-all-start.1 = ((bf16[8,12,1280]{2,1,0:T(8,128)(2,1)}), bf16[8,12,1280]{2,1,0:T(8,128)(2,1)}, u32[]{:S(2)}, u32[]{:S(2)}) async-start(bf16[8,12,1280]{2,1,0:T(8,128)(2,1)} %copy.66), calls=%async_computation.1 | async-start | bytes 655360 | tf_op jit(solution)/shard_map/all_to_all | solution.py:191
  46.9 2.1 %collective-permute-start.1 = (bf16[96,1280]{1,0:T(8,128)(2,1)S(1)}, bf16[96,1280]{1,0:T(8,128)(2,1)S(1)}, u32[]{:S(2)}, u32[]{:S(2)}) collective-permute-start(bf16[96,1280]{1,0:T(8,128)(2,1)S(1)} %pad_maximum_fusion.4), channel_id=1, source_target_pairs={{0,4},{4,0},{8,12},{12,8},{16,20},{20,16},{24,28},{28,24},{1,5},{5... | collective-permute-start | bytes 737288 | tf_op jit(solution)/shard_map/ppermute | solution.py:118
  53.0 2.6 %collective-permute-done.1 = bf16[96,1280]{1,0:T(8,128)(2,1)S(1)} collective-permute-done((bf16[96,1280]{1,0:T(8,128)(2,1)S(1)}, bf16[96,1280]{1,0:T(8,128)(2,1)S(1)}, u32[]{:S(2)}, u32[]{:S(2)}) %collective-permute-start.1) | collective-permute-done | bytes 245792 | tf_op jit(solution)/shard_map/ppermute | solution.py:118
  68.0 2.1 %collective-permute-start.13 = (bf16[48,1280]{1,0:T(8,128)(2,1)S(1)}, bf16[48,1280]{1,0:T(8,128)(2,1)S(1)}, u32[]{:S(2)}, u32[]{:S(2)}) collective-permute-start(bf16[48,1280]{1,0:T(8,128)(2,1)S(1)} %reshape.795), channel_id=1, source_target_pairs={{0,16},{4,20},{8,24},{12,28},{16,0},{20,4},{24,8},{28,12},{1,17},{... | collective-permute-start | bytes 368648 | tf_op jit(solution)/shard_map/ppermute | solution.py:113
  71.4 2.7 %collective-permute-done.10 = bf16[48,1280]{1,0:T(8,128)(2,1)S(1)} collective-permute-done((bf16[48,1280]{1,0:T(8,128)(2,1)S(1)}, bf16[48,1280]{1,0:T(8,128)(2,1)S(1)}, u32[]{:S(2)}, u32[]{:S(2)}) %collective-permute-start.10) | collective-permute-done | bytes 122912 | tf_op jit(solution)/shard_map/ppermute | solution.py:113
  75.2 2.1 %collective-permute-done.13 = bf16[48,1280]{1,0:T(8,128)(2,1)S(1)} collective-permute-done((bf16[48,1280]{1,0:T(8,128)(2,1)S(1)}, bf16[48,1280]{1,0:T(8,128)(2,1)S(1)}, u32[]{:S(2)}, u32[]{:S(2)}) %collective-permute-start.13) | collective-permute-done | bytes 122912 | tf_op jit(solution)/shard_map/ppermute | solution.py:113
  89.4 8.9 %collective-permute-done.12 = bf16[192,1280]{1,0:T(8,128)(2,1)S(1)} collective-permute-done((bf16[192,1280]{1,0:T(8,128)(2,1)S(1)}, bf16[192,1280]{1,0:T(8,128)(2,1)S(1)}, u32[]{:S(2)}, u32[]{:S(2)}) %collective-permute-start.12) | collective-permute-done | bytes 491552 | tf_op jit(solution)/shard_map/ppermute | solution.py:118
  106.4 7.7 %multiply_reduce_fusion = (f32[1280]{0:T(1024)S(1)}, f32[384,1280]{1,0:T(8,128)}) fusion(f32[8,48,1280]{2,1,0:T(8,128)} %copy.61, f32[384]{0:T(512)S(1)} %copy-done.12, f32[384]{0:T(512)S(1)} %copy-done.14, bf16[1280,1280]{1,0:T(8,128)(2,1)S(1)} %copy-done, bf16[384,1280]{1,0:T(8,128)(2,1)} %fusion.2, bf16[1280,1280]{1,0:T(8,128)(2,1)} %param.12, ...), kind=kOutput, calls=%fused_computation.22 | convolution fusion | flops 2527394560 | bytes 13443072 | tf_op jit(solution)/shard_map/dot_general | solution.py:36
  117.0 6.1 %fusion.70 = f32[768,1280]{1,0:T(8,128)} fusion(bf16[768,1280]{1,0:T(8,128)(2,1)} %constant_dynamic-update-slice_fusion.8, bf16[1280,1280]{1,0:T(8,128)(2,1)S(1)} %copy-done), kind=kOutput, calls=%fused_computation.155 | convolution fusion | flops 2516582400 | bytes 9175040 | tf_op jit(solution)/shard_map/dot_general | solution.py:32
  123.1 2.8 %reshape.794 = f32[8,2,2,12,1280]{4,3,2,1,0:T(8,128)} reshape(f32[384,1280]{1,0:T(8,128)} %get-tuple-element.15) | data formatting | bytes 3932160 | tf_op jit(solution)/shard_map/reshape | solution.py:220
  127.8 2.5 %constant_dynamic-slice_fusion = f32[8,2,1,12,1280]{4,3,2,1,0:T(8,128)} fusion(f32[8,2,2,12,1280]{4,3,2,1,0:T(8,128)} %reshape.794, s32[]{:T(128)S(6)} %select_n.173), kind=kLoop, calls=%fused_computation.103 | loop fusion | bytes 1966084 | tf_op jit(solution)/shard_map/jit(dynamic_index_in_dim)/dynamic_slice | solution.py:223
  134.0 2.5 %collective-permute-start.22 = (f32[1280]{0:T(1024)S(1)}, f32[1280]{0:T(1024)S(1)}, u32[]{:S(2)}, u32[]{:S(2)}) collective-permute-start(f32[1280]{0:T(1024)S(1)} %add.299), channel_id=1, source_target_pairs={{0,16},{4,20},{8,24},{12,28},{16,0},{20,4},{24,8},{28,12},{1,17},{... | collective-permute-start | bytes 15368 | tf_op jit(solution)/shard_map/ppermute | solution.py:118
  139.9 6.1 %fusion.71 = f32[768,1280]{1,0:T(8,128)} fusion(bf16[768,1280]{1,0:T(8,128)(2,1)} %collective-permute-done.17, bf16[1280,1280]{1,0:T(8,128)(2,1)S(1)} %copy-done), kind=kOutput, calls=%fused_computation.156 | convolution fusion | flops 2516582400 | bytes 9175040 | tf_op jit(solution)/shard_map/dot_general | solution.py:32
  146.1 9.0 %fusion.6 = f32[160,1280]{1,0:T(8,128)} fusion(f32[768,1280]{1,0:T(8,128)} %fusion.71, bf16[768,1280]{1,0:T(8,128)(2,1)} %copy-done.18, bf16[1280,1280]{1,0:T(8,128)(2,1)} %param.12, bf16[768,1280]{1,0:T(8,128)(2,1)} %collective-permute-done.17, s32[]{:T(128)S(6)} %select_n.178), kind=kOutput, calls=%fused_computation.29 | convolution fusion | flops 2848849920 | bytes 10387460 | tf_op jit(solution)/shard_map/dot_general | solution.py:40
  155.0 9.1 %convolution_add_fusion.2 = f32[160,1280]{1,0:T(8,128)} fusion(f32[160,1280]{1,0:T(8,128)} %fusion.6, f32[768,1280]{1,0:T(8,128)} %fusion.70, bf16[768,1280]{1,0:T(8,128)(2,1)} %constant_dynamic-update-slice_fusion, bf16[1280,1280]{1,0:T(8,128)(2,1)} %param.12, bf16[768,1280]{1,0:T(8,128)(2,1)} %constant_dynamic-update-slice_fusion.8, s32[]{:T(128)S(6)} %select_n.178), kind=kOutput, calls=%fused_computation.17 | convolution fusion | flops 2849054720 | bytes 11206660 | tf_op jit(solution)/shard_map/dot_general | solution.py:40
  164.1 4.0 %fusion.5 = f32[1280,160]{0,1:T(8,128)S(1)} fusion(f32[768,1280]{1,0:T(8,128)} %fusion.71, bf16[768,1280]{1,0:T(8,128)(2,1)} %copy-done.18, s32[]{:T(128)S(6)} %select_n.178), kind=kOutput, calls=%fused_computation.25 | convolution fusion | flops 323420160 | bytes 5144580 | tf_op jit(solution)/shard_map/dot_general | solution.py:40
  170.7 3.6 %convolution_add_fusion.1 = f32[1280,160]{0,1:T(8,128)} fusion(f32[1280,160]{0,1:T(8,128)S(1)} %fusion.5, f32[768,1280]{1,0:T(8,128)S(1)} %copy-done.19, bf16[768,1280]{1,0:T(8,128)(2,1)} %constant_dynamic-update-slice_fusion, s32[]{:T(128)S(6)} %select_n.178), kind=kOutput, calls=%fused_computation.16 | convolution fusion | flops 323624960 | bytes 5963780 | tf_op jit(solution)/shard_map/dot_general | solution.py:40
  174.3 4.2 %collective-permute-done.9 = bf16[8,12,1280]{2,0,1:T(8,128)(2,1)S(1)} collective-permute-done((bf16[8,12,1280]{2,0,1:T(8,128)(2,1)S(1)}, bf16[8,12,1280]{2,0,1:T(8,128)(2,1)S(1)}, u32[]{:S(2)}, u32[]{:S(2)}) %collective-permute-start.9) | collective-permute-done | bytes 245792 | tf_op jit(solution)/shard_map/ppermute | solution.py:118
  (152 shorter events, 76.1 us)
Async XLA Ops:
  3.3 42.6 %collective-permute-start = (bf16[48,1280]{1,0:T(8,128)(2,1)S(1)}, bf16[48,1280]{1,0:T(8,128)(2,1)}, u32[]{:S(2)}, u32[]{:S(2)}) collective-permute-start(bf16[48,1280]{1,0:T(8,128)(2,1)S(1)} %reshape.792), channel_id=1, source_target_pairs={{0,8},{4,12},{8,16},{12,20},{16,24},{20,28},{24,0},{28,4},{1,9},{5... | collective-permute-start | bytes 368648 | tf_op jit(solution)/shard_map/ppermute | solution.py:113
  6.4 42.6 %collective-permute-start.3 = (bf16[48,1280]{1,0:T(8,128)(2,1)S(1)}, bf16[48,1280]{1,0:T(8,128)(2,1)S(1)}, u32[]{:S(2)}, u32[]{:S(2)}) collective-permute-start(bf16[48,1280]{1,0:T(8,128)(2,1)S(1)} %reshape.792), channel_id=1, source_target_pairs={{0,16},{4,20},{8,24},{12,28},{16,0},{20,4},{24,8},{28,12},{1,17},{... | collective-permute-start | bytes 368648 | tf_op jit(solution)/shard_map/ppermute | solution.py:113
  9.0 40.0 %collective-permute-start.4 = (bf16[48,1280]{1,0:T(8,128)(2,1)S(1)}, bf16[48,1280]{1,0:T(8,128)(2,1)}, u32[]{:S(2)}, u32[]{:S(2)}) collective-permute-start(bf16[48,1280]{1,0:T(8,128)(2,1)S(1)} %reshape.792), channel_id=1, source_target_pairs={{0,24},{4,28},{8,0},{12,4},{16,8},{20,12},{24,16},{28,20},{1,25},{... | collective-permute-start | bytes 368648 | tf_op jit(solution)/shard_map/ppermute | solution.py:113
  13.2 21.9 %all-to-all-start = ((s32[8,1,1]{2,1,0:T(1,128)}), s32[8,1,1]{2,1,0:T(1,128)}, u32[]{:S(2)}, u32[]{:S(2)}) async-start(s32[8,1,1]{2,1,0:T(1,128)} %copy.57), calls=%async_computation | async-start | bytes 8192 | tf_op jit(solution)/shard_map/all_to_all | solution.py:175
  38.8 24.3 %all-to-all-start.1 = ((bf16[8,12,1280]{2,1,0:T(8,128)(2,1)}), bf16[8,12,1280]{2,1,0:T(8,128)(2,1)}, u32[]{:S(2)}, u32[]{:S(2)}) async-start(bf16[8,12,1280]{2,1,0:T(8,128)(2,1)} %copy.66), calls=%async_computation.1 | async-start | bytes 655360 | tf_op jit(solution)/shard_map/all_to_all | solution.py:191
  46.9 8.7 %collective-permute-start.1 = (bf16[96,1280]{1,0:T(8,128)(2,1)S(1)}, bf16[96,1280]{1,0:T(8,128)(2,1)S(1)}, u32[]{:S(2)}, u32[]{:S(2)}) collective-permute-start(bf16[96,1280]{1,0:T(8,128)(2,1)S(1)} %pad_maximum_fusion.4), channel_id=1, source_target_pairs={{0,4},{4,0},{8,12},{12,8},{16,20},{20,16},{24,28},{28,24},{1,5},{5... | collective-permute-start | bytes 737288 | tf_op jit(solution)/shard_map/ppermute | solution.py:118
  49.9 8.9 %collective-permute-start.5 = (bf16[96,1280]{1,0:T(8,128)(2,1)S(1)}, bf16[96,1280]{1,0:T(8,128)(2,1)S(1)}, u32[]{:S(2)}, u32[]{:S(2)}) collective-permute-start(bf16[96,1280]{1,0:T(8,128)(2,1)S(1)} %pad_maximum_fusion.5), channel_id=1, source_target_pairs={{0,2},{1,3},{2,0},{3,1},{4,6},{5,7},{6,4},{7,5},{8,10},{9,11},{10,... | collective-permute-start | bytes 737288 | tf_op jit(solution)/shard_map/ppermute | solution.py:118
  57.4 20.5 %collective-permute-start.2 = (bf16[192,1280]{1,0:T(8,128)(2,1)}, bf16[192,1280]{1,0:T(8,128)(2,1)}, u32[]{:S(2)}, u32[]{:S(2)}) collective-permute-start(bf16[192,1280]{1,0:T(8,128)(2,1)} %pad_maximum_fusion), channel_id=1, source_target_pairs={{0,2},{1,3},{2,0},{3,1},{4,6},{5,7},{6,4},{7,5},{8,10},{9,11},{10,... | collective-permute-start | bytes 1474568 | tf_op jit(solution)/shard_map/ppermute | solution.py:118
  61.3 21.4 %collective-permute-start.6 = (bf16[192,1280]{1,0:T(8,128)(2,1)}, bf16[192,1280]{1,0:T(8,128)(2,1)}, u32[]{:S(2)}, u32[]{:S(2)}) collective-permute-start(bf16[192,1280]{1,0:T(8,128)(2,1)} %pad_maximum_fusion.1), channel_id=1, source_target_pairs={{0,4},{4,0},{8,12},{12,8},{16,20},{20,16},{24,28},{28,24},{1,5},{5... | collective-permute-start | bytes 1474568 | tf_op jit(solution)/shard_map/ppermute | solution.py:118
  66.0 8.1 %collective-permute-start.10 = (bf16[48,1280]{1,0:T(8,128)(2,1)S(1)}, bf16[48,1280]{1,0:T(8,128)(2,1)S(1)}, u32[]{:S(2)}, u32[]{:S(2)}) collective-permute-start(bf16[48,1280]{1,0:T(8,128)(2,1)S(1)} %reshape.795), channel_id=1, source_target_pairs={{0,8},{4,12},{8,16},{12,20},{16,24},{20,28},{24,0},{28,4},{1,9},{5... | collective-permute-start | bytes 368648 | tf_op jit(solution)/shard_map/ppermute | solution.py:113
  68.0 9.3 %collective-permute-start.13 = (bf16[48,1280]{1,0:T(8,128)(2,1)S(1)}, bf16[48,1280]{1,0:T(8,128)(2,1)S(1)}, u32[]{:S(2)}, u32[]{:S(2)}) collective-permute-start(bf16[48,1280]{1,0:T(8,128)(2,1)S(1)} %reshape.795), channel_id=1, source_target_pairs={{0,16},{4,20},{8,24},{12,28},{16,0},{20,4},{24,8},{28,12},{1,17},{... | collective-permute-start | bytes 368648 | tf_op jit(solution)/shard_map/ppermute | solution.py:113
  70.0 7.2 %collective-permute-start.14 = (bf16[48,1280]{1,0:T(8,128)(2,1)S(1)}, bf16[48,1280]{1,0:T(8,128)(2,1)S(1)}, u32[]{:S(2)}, u32[]{:S(2)}) collective-permute-start(bf16[48,1280]{1,0:T(8,128)(2,1)S(1)} %reshape.795), channel_id=1, source_target_pairs={{0,24},{4,28},{8,0},{12,4},{16,8},{20,12},{24,16},{28,20},{1,25},{... | collective-permute-start | bytes 368648 | tf_op jit(solution)/shard_map/ppermute | solution.py:113
  74.1 10.4 %collective-permute-start.11 = (bf16[96,1280]{1,0:T(8,128)(2,1)S(1)}, bf16[96,1280]{1,0:T(8,128)(2,1)S(1)}, u32[]{:S(2)}, u32[]{:S(2)}) collective-permute-start(bf16[96,1280]{1,0:T(8,128)(2,1)S(1)} %pad_maximum_fusion.6), channel_id=1, source_target_pairs={{0,4},{4,0},{8,12},{12,8},{16,20},{20,16},{24,28},{28,24},{1,5},{5... | collective-permute-start | bytes 737288 | tf_op jit(solution)/shard_map/ppermute | solution.py:118
  77.3 9.5 %collective-permute-start.15 = (bf16[96,1280]{1,0:T(8,128)(2,1)S(1)}, bf16[96,1280]{1,0:T(8,128)(2,1)S(1)}, u32[]{:S(2)}, u32[]{:S(2)}) collective-permute-start(bf16[96,1280]{1,0:T(8,128)(2,1)S(1)} %pad_maximum_fusion.7), channel_id=1, source_target_pairs={{0,2},{1,3},{2,0},{3,1},{4,6},{5,7},{6,4},{7,5},{8,10},{9,11},{10,... | collective-permute-start | bytes 737288 | tf_op jit(solution)/shard_map/ppermute | solution.py:118
  84.6 17.4 %collective-permute-start.7 = (bf16[768,1280]{1,0:T(8,128)(2,1)}, bf16[768,1280]{1,0:T(8,128)(2,1)S(1)}, u32[]{:S(2)}, u32[]{:S(2)}) collective-permute-start(bf16[768,1280]{1,0:T(8,128)(2,1)} %constant_dynamic-update-slice_fusion), channel_id=1, source_target_pairs={{0,1},{1,0},{2,3},{3,2},{4,5},{5,4},{6,7},{7,6},{8,9},{9,8},{10,11... | collective-permute-start | bytes 5898248 | tf_op jit(solution)/shard_map/ppermute | solution.py:118
  84.6 13.7 %collective-permute-start.12 = (bf16[192,1280]{1,0:T(8,128)(2,1)S(1)}, bf16[192,1280]{1,0:T(8,128)(2,1)S(1)}, u32[]{:S(2)}, u32[]{:S(2)}) collective-permute-start(bf16[192,1280]{1,0:T(8,128)(2,1)S(1)} %pad_maximum_fusion.2), channel_id=1, source_target_pairs={{0,2},{1,3},{2,0},{3,1},{4,6},{5,7},{6,4},{7,5},{8,10},{9,11},{10,... | collective-permute-start | bytes 1474568 | tf_op jit(solution)/shard_map/ppermute | solution.py:118
  86.8 14.3 %collective-permute-start.16 = (bf16[192,1280]{1,0:T(8,128)(2,1)S(1)}, bf16[192,1280]{1,0:T(8,128)(2,1)S(1)}, u32[]{:S(2)}, u32[]{:S(2)}) collective-permute-start(bf16[192,1280]{1,0:T(8,128)(2,1)S(1)} %pad_maximum_fusion.3), channel_id=1, source_target_pairs={{0,4},{4,0},{8,12},{12,8},{16,20},{20,16},{24,28},{28,24},{1,5},{5... | collective-permute-start | bytes 1474568 | tf_op jit(solution)/shard_map/ppermute | solution.py:118
  102.0 38.0 %collective-permute-start.17 = (bf16[768,1280]{1,0:T(8,128)(2,1)}, bf16[768,1280]{1,0:T(8,128)(2,1)}, u32[]{:S(2)}, u32[]{:S(2)}) collective-permute-start(bf16[768,1280]{1,0:T(8,128)(2,1)} %constant_dynamic-update-slice_fusion.8), channel_id=1, source_target_pairs={{0,1},{1,0},{2,3},{3,2},{4,5},{5,4},{6,7},{7,6},{8,9},{9,8},{10,11... | collective-permute-start | bytes 5898248 | tf_op jit(solution)/shard_map/ppermute | solution.py:118
  115.5 10.4 %collective-permute-start.19 = (f32[1280]{0:T(1024)S(1)}, f32[1280]{0:T(1024)S(1)}, u32[]{:S(2)}, u32[]{:S(2)}) collective-permute-start(f32[1280]{0:T(1024)S(1)} %add.296), channel_id=1, source_target_pairs={{0,2},{1,3},{2,0},{3,1},{4,6},{5,7},{6,4},{7,5},{8,10},{9,11},{10,... | collective-permute-start | bytes 15368 | tf_op jit(solution)/shard_map/ppermute | solution.py:118
  126.0 4.3 %collective-permute-start.20 = (f32[1280]{0:T(1024)S(1)}, f32[1280]{0:T(1024)S(1)}, u32[]{:S(2)}, u32[]{:S(2)}) collective-permute-start(f32[1280]{0:T(1024)S(1)} %add.297), channel_id=1, source_target_pairs={{0,4},{4,0},{8,12},{12,8},{16,20},{20,16},{24,28},{28,24},{1,5},{5... | collective-permute-start | bytes 15368 | tf_op jit(solution)/shard_map/ppermute | solution.py:118
  130.3 3.7 %collective-permute-start.21 = (f32[1280]{0:T(1024)S(1)}, f32[1280]{0:T(1024)S(1)}, u32[]{:S(2)}, u32[]{:S(2)}) collective-permute-start(f32[1280]{0:T(1024)S(1)} %add.298), channel_id=1, source_target_pairs={{0,8},{4,12},{8,0},{12,4},{16,24},{20,28},{24,16},{28,20},{1,9},{5... | collective-permute-start | bytes 15368 | tf_op jit(solution)/shard_map/ppermute | solution.py:118
  134.0 5.4 %collective-permute-start.22 = (f32[1280]{0:T(1024)S(1)}, f32[1280]{0:T(1024)S(1)}, u32[]{:S(2)}, u32[]{:S(2)}) collective-permute-start(f32[1280]{0:T(1024)S(1)} %add.299), channel_id=1, source_target_pairs={{0,16},{4,20},{8,24},{12,28},{16,0},{20,4},{24,8},{28,12},{1,17},{... | collective-permute-start | bytes 15368 | tf_op jit(solution)/shard_map/ppermute | solution.py:118
  139.3 28.8 %collective-permute-start.8 = (bf16[8,2,12,1280]{3,0,2,1:T(8,128)(2,1)}, bf16[8,2,12,1280]{3,0,2,1:T(8,128)(2,1)}, u32[]{:S(2)}, u32[]{:S(2)}) collective-permute-start(bf16[8,2,12,1280]{3,0,2,1:T(8,128)(2,1)} %copy.65), channel_id=1, source_target_pairs={{0,1},{1,0},{2,3},{3,2},{4,5},{5,4},{6,7},{7,6},{8,9},{9,8},{10,11... | collective-permute-start | bytes 1474568 | tf_op jit(solution)/shard_map/ppermute | solution.py:118
  170.1 8.4 %collective-permute-start.9 = (bf16[8,12,1280]{2,0,1:T(8,128)(2,1)S(1)}, bf16[8,12,1280]{2,0,1:T(8,128)(2,1)S(1)}, u32[]{:S(2)}, u32[]{:S(2)}) collective-permute-start(bf16[8,12,1280]{2,0,1:T(8,128)(2,1)S(1)} %fusion.17), channel_id=1, source_target_pairs={{0,2},{1,3},{2,0},{3,1},{4,6},{5,7},{6,4},{7,5},{8,10},{9,11},{10,... | collective-permute-start | bytes 737288 | tf_op jit(solution)/shard_map/ppermute | solution.py:118
  (21 other events, 148.4 us)
